TPU v7x, 32 devices: a whole 2x2x4 slice. The times are simulated.
32 devices in a mesh: groups: 2 (over x), gx: 16 (over z, y, core).
Axes of the slice: x: 2, y: 2, z: 4, core: 2. Of those that a mesh axis runs over, the one named last changes fastest.
Arguments:
- volume: bfloat16 [32, 256, 6, 128], P('groups', 'gx'), parts along dimension 0, may hold values from -6 to 6
- conv_weight: bfloat16 [256, 27, 128], P('gx'), may hold values from -0.078125 to 0.078125
- conv_bias: float32 [128], replicated, may hold values from -3 to 3
- tconv_weight: bfloat16 [27, 64, 128], replicated, may hold values from -0.25 to 0.25
Outputs:
- decoded: bfloat16 [64, 64, 12, 256], P(('groups', 'gx')), parts along dimension 0
There are 2 independent parts, one for each index of `groups`. A program takes and returns all parts, laid end to end along the dimension named above; an argument that names none is the same for every part. Nothing has to cross between parts.
All inputs are finite; a program needn't handle non-finite values.
Results may differ from a plain program's by a relative error of at most 0.005.
Values may be sent and summed in bfloat16 or wider, within the bound.
A program may use at most 64 MiB of HBM per device.

v0:
```python
import jax
import jax.numpy as jnp
from jax import lax
from jax.sharding import PartitionSpec as P


def extended(block, sides, width):
    for axis, dim in sides:
        count = lax.axis_size(axis)
        forward = [(i, i + 1) for i in range(count - 1)]
        backward = [(target, source) for source, target in forward]
        low = lax.ppermute(
            lax.slice_in_dim(block, block.shape[dim] - width, None, axis=dim), axis, forward
        )
        high = lax.ppermute(lax.slice_in_dim(block, 0, width, axis=dim), axis, backward)
        block = jnp.concatenate([low, block, high], axis=dim)
    return block


def from_behind(block, axis, distance):
    devices = range(lax.axis_size(axis))
    route = [(i - distance, i) for i in devices if i - distance in devices]
    return lax.ppermute(block, axis, route)


def next_cell(field, axis):
    size = field.shape[axis]
    rest = lax.slice_in_dim(field, 1, size, axis=axis)
    zero_shape = list(field.shape)
    zero_shape[axis] = 1
    return jnp.concatenate([rest, jnp.zeros(zero_shape, field.dtype)], axis=axis)


def yz_classes(products, tap_x):
    layout_options = (((1, False),), ((2, False), (0, True)))
    parity_classes = []
    for par_y in range(2):
        for par_z in range(2):
            total = jnp.zeros(products.shape[:1] + products.shape[4:], jnp.float32)
            for tap_y, shift_y in layout_options[par_y]:
                for tap_z, shift_z in layout_options[par_z]:
                    term = products[:, tap_x, tap_y, tap_z]
                    if shift_y:
                        term = next_cell(term, 2)
                    if shift_z:
                        term = next_cell(term, 3)
                    total = total + term
            parity_classes.append(total)
    return jnp.stack(parity_classes, axis=0)


def alternate(even, odd):
    both = jnp.stack([even, odd], axis=0)
    rows, chans, wide_y, wide_z = (both.shape[2], both.shape[3], both.shape[4], both.shape[5])
    both = both.reshape(2, 2, 2, rows, chans, wide_y, wide_z)
    both = jnp.transpose(both, (3, 0, 4, 5, 1, 6, 2))
    return both.reshape(2 * rows, chans, 2 * wide_y, 2 * wide_z)


def conv_rows(block, weight, count):
    chans, wide_y, wide_z = (block.shape[1], block.shape[2] - 2, block.shape[3] - 2)
    taps = []
    for tap_x in range(3):
        for tap_y in range(3):
            for tap_z in range(3):
                taps.append(
                    block[tap_x : tap_x + count, :, tap_y : tap_y + wide_y, tap_z : tap_z + wide_z]
                )
    patch_columns = jnp.stack(taps, axis=2).reshape(count, chans * 27, wide_y * wide_z)
    flattened_patches = weight.reshape(chans * 27, weight.shape[2])
    output_volume = jnp.einsum(
        "fwh,wb->fbh", patch_columns, flattened_patches, preferred_element_type=jnp.float32
    )
    return output_volume.reshape(count, weight.shape[2], wide_y, wide_z)


def tap_products(hidden, flattened_patches, cup):
    rows, wide_y, wide_z = (hidden.shape[0], hidden.shape[2], hidden.shape[3])
    products = jnp.einsum(
        "oc,ncyz->noyz", flattened_patches, hidden, preferred_element_type=jnp.float32
    )
    return products.reshape(rows, 3, 3, 3, cup, wide_y, wide_z)


def per_device(volume, conv_weight, conv_bias, tconv_weight):
    wide_x, wide_y, wide_z = (volume.shape[0], volume.shape[2], volume.shape[3])
    rows = wide_x // lax.axis_size("gx")
    cout = conv_weight.shape[2]
    local = lax.all_to_all(volume, "gx", split_axis=0, concat_axis=1, tiled=True)
    widened_volume = extended(local, (("gx", 0),), 1)
    padded_volume = jnp.pad(widened_volume, ((0, 0), (0, 0), (1, 1), (1, 1)))
    summed = conv_rows(padded_volume, lax.all_gather(conv_weight, "gx", axis=0, tiled=True), rows)
    hidden = jnp.maximum(summed + conv_bias[None, :, None, None], 0.0).astype(jnp.bfloat16)
    cup = tconv_weight.shape[1]
    flattened_patches = tconv_weight.reshape(27 * cup, cout)
    products = tap_products(hidden, flattened_patches, cup)
    first = yz_classes(products, 0)
    middle = yz_classes(products, 1)
    last = yz_classes(products, 2)
    edge = from_behind(hidden, "gx", -1)
    leading_edge = yz_classes(tap_products(edge, flattened_patches, cup), 0)
    following = jnp.concatenate([first[:, 1:], leading_edge], axis=1)
    odd = last + following
    return alternate(middle, odd).astype(jnp.bfloat16)


def solution(mesh):
    return jax.shard_map(
        per_device,
        mesh=mesh,
        in_specs=(P("groups", "gx", None, None), P("gx", None, None), P(), P()),
        out_specs=P(("groups", "gx"), None, None, None),
        check_vma=False,
    )
```

profile of v0, /device:TPU:5, one launch (start us, length us, event | category | flops | bytes accessed | tf_op | source)
XLA Modules:
  0.0 140.1 jit_solution(13895225849409607237)
XLA Ops:
  6.5 0.0 copy-start
  6.5 0.0 all-gather.2.cloned.1.call-start
  6.5 17.9 %all_to_all.12 = bf16[16,16,6,128]{3,1,2,0:T(8,128)(2,1)S(1)} all-to-all(bf16[16,16,6,128]{3,1,2,0:T(8,128)(2,1)} %param.4), channel_id=1, replica_groups=mesh['groups'=2,'gx'=16] {'gx'}, dimensions={0} | all-to-all | bytes 786432 | tf_op jit(solution)/shard_map/all_to_all | solution.py:89
  24.4 3.2 %collective-permute-start = (bf16[1,256,6,128]{3,1,2,0:T(8,128)(2,1)S(1)}, bf16[1,256,6,128]{3,1,2,0:T(8,128)(2,1)S(1)}, u32[]{:S(2)}, u32[]{:S(2)}) collective-permute-start(bf16[1,256,6,128]{3,1,2,0:T(8,128)(2,1)S(1)} %bitcast.296), channel_id=1, source_target_pairs={{0,1},{1,2},{2,3},{3,4},{4,5},{5,6},{6,7},{7,8},{8,9},{9,10},{10,1... | collective-permute-start | bytes 1179656 | tf_op jit(solution)/shard_map/ppermute | solution.py:12
  27.7 1.9 %collective-permute-start.1 = (bf16[1,256,6,128]{3,1,2,0:T(8,128)(2,1)S(1)}, bf16[1,256,6,128]{3,1,2,0:T(8,128)(2,1)S(1)}, u32[]{:S(2)}, u32[]{:S(2)}) collective-permute-start(bf16[1,256,6,128]{3,1,2,0:T(8,128)(2,1)S(1)} %bitcast.297), channel_id=1, source_target_pairs={{1,0},{2,1},{3,2},{4,3},{5,4},{6,5},{7,6},{8,7},{9,8},{10,9},{11,1... | collective-permute-start | bytes 1179656 | tf_op jit(solution)/shard_map/ppermute | solution.py:15
  29.6 0.0 all-gather.2.cloned.1.call-update
  29.6 2.8 %collective-permute-done = bf16[1,256,6,128]{3,1,2,0:T(8,128)(2,1)S(1)} collective-permute-done((bf16[1,256,6,128]{3,1,2,0:T(8,128)(2,1)S(1)}, bf16[1,256,6,128]{3,1,2,0:T(8,128)(2,1)S(1)}, u32[]{:S(2)}, u32[]{:S(2)}) %collective-permute-start) | collective-permute-done | bytes 393248 | tf_op jit(solution)/shard_map/ppermute | solution.py:12
  32.4 5.3 %collective-permute-done.1 = bf16[1,256,6,128]{3,1,2,0:T(8,128)(2,1)S(1)} collective-permute-done((bf16[1,256,6,128]{3,1,2,0:T(8,128)(2,1)S(1)}, bf16[1,256,6,128]{3,1,2,0:T(8,128)(2,1)S(1)}, u32[]{:S(2)}, u32[]{:S(2)}) %collective-permute-start.1) | collective-permute-done | bytes 393248 | tf_op jit(solution)/shard_map/ppermute | solution.py:15
  37.7 1.7 %select_maximum_fusion = bf16[3,256,8,130]{3,1,2,0:T(8,128)(2,1)S(1)} fusion(bf16[1,256,6,128]{3,1,2,0:T(8,128)(2,1)S(1)} %collective-permute-done.1, bf16[1,256,6,128]{3,1,2,0:T(8,128)(2,1)S(1)} %bitcast.298, bf16[1,256,6,128]{3,1,2,0:T(8,128)(2,1)S(1)} %collective-permute-done), kind=kLoop, calls=%fused_computation.8 | loop fusion | flops 15175680 | bytes 2777088 | tf_op jit(solution)/shard_map/concatenate | solution.py:16
  39.4 0.1 fusion.32
  39.5 0.2 fusion.31
  39.7 0.2 fusion.30
  40.0 0.1 fusion.29
  40.1 0.1 bitcast_dynamic-update-slice_fusion.1
  40.1 0.2 fusion.28
  40.4 0.1 fusion.27
  40.5 0.2 fusion.26
  40.7 0.2 fusion.25
  41.0 0.1 fusion.24
  41.1 0.2 fusion.23
  41.3 0.2 fusion.22
  41.6 0.1 fusion.21
  41.7 0.1 constant_dynamic-update-slice_fusion
  41.7 0.2 fusion.20
  42.0 0.1 fusion.19
  42.1 0.2 fusion.18
  42.3 0.2 fusion.17
  42.6 0.1 fusion.16
  42.7 0.2 fusion.15
  42.9 0.2 fusion.14
  43.2 0.1 fusion.13
  43.3 0.1 bitcast_dynamic-update-slice_fusion
  43.3 0.2 fusion.12
  43.6 0.1 fusion.11
  43.7 0.2 fusion.10
  43.9 0.2 fusion.9
  44.2 43.2 %copy.129 = bf16[1,256,27,6,128]{4,3,2,1,0:T(8,128)(2,1)S(1)} copy(bf16[1,256,27,6,128]{4,1,3,2,0:T(8,128)(2,1)S(1)} %fusion.9) | data formatting | bytes 21233664 | tf_op jit(solution)/shard_map/stack | solution.py:69
  87.3 6.4 %copy.252 = bf16[864,8,6,128]{3,1,2,0:T(8,128)(2,1)} copy(bf16[864,8,6,128]{3,2,1,0:T(8,128)(2,1)S(1)} %bitcast.288) | data formatting | bytes 21233664
  93.8 13.9 %copy.130 = bf16[768,6912]{1,0:T(8,128)(2,1)} copy(bf16[768,6912]{0,1:T(8,128)(2,1)} %bitcast.289) | data formatting | bytes 21233664 | tf_op jit(solution)/shard_map/fwh,wb->fbh/dot_general | solution.py:71
  107.7 2.7 %copy.131 = bf16[256,27,128]{2,1,0:T(8,128)(2,1)S(1)} copy(bf16[256,27,128]{2,0,1:T(8,128)(2,1)} %all-gather.2.cloned.1.call-done) | data formatting | bytes 3538944 | tf_op jit(solution)/shard_map/all_gather | solution.py:92
  110.3 1.6 %reshape.119 = bf16[6912,128,1]{1,0,2:T(8,128)(2,1)} reshape(bf16[256,27,128]{2,1,0:T(8,128)(2,1)S(1)} %copy.131) | data formatting | bytes 3538944 | tf_op jit(solution)/shard_map/reshape | solution.py:70
  111.9 7.4 %fusion.7 = bf16[6,128,128]{2,1,0:T(8,128)(2,1)S(1)} fusion(bf16[6,128,6912]{2,1,0:T(8,128)(2,1)} %bitcast.292, bf16[6912,128,1]{1,0,2:T(8,128)(2,1)} %reshape.119, f32[128]{0:T(128)S(1)} %copy-done.1), kind=kOutput, calls=%fused_computation.15 | convolution fusion | flops 1359249408 | bytes 12583424 | tf_op jit(solution)/shard_map/fwh,wb->fbh/dot_general | solution.py:71
  119.3 0.9 fusion.59
  120.2 0.4 fusion.65
  120.7 0.1 slice.310
  120.9 0.1 slice.316
  121.0 0.1 pad_slice_fusion.2
  121.2 1.9 %collective-permute-start.2 = (bf16[1,128,6,128]{1,3,2,0:T(8,128)(2,1)S(1)}, bf16[1,128,6,128]{1,3,2,0:T(8,128)(2,1)S(1)}, u32[]{:S(2)}, u32[]{:S(2)}) collective-permute-start(bf16[1,128,6,128]{1,3,2,0:T(8,128)(2,1)S(1)} %bitcast.303), channel_id=1, source_target_pairs={{1,0},{2,1},{3,2},{4,3},{5,4},{6,5},{7,6},{8,7},{9,8},{10,9},{11,1... | collective-permute-start | bytes 589832 | tf_op jit(solution)/shard_map/ppermute | solution.py:23
  123.1 0.1 slice.324
  123.3 0.1 slice.330
  123.4 0.1 pad_slice_fusion.1
  123.7 0.1 fusion.64
  123.8 0.1 pad_maximum_fusion
  123.9 5.2 %collective-permute-done.2 = bf16[1,128,6,128]{1,3,2,0:T(8,128)(2,1)S(1)} collective-permute-done((bf16[1,128,6,128]{1,3,2,0:T(8,128)(2,1)S(1)}, bf16[1,128,6,128]{1,3,2,0:T(8,128)(2,1)S(1)}, u32[]{:S(2)}, u32[]{:S(2)}) %collective-permute-start.2) | collective-permute-done | bytes 196640 | tf_op jit(solution)/shard_map/ppermute | solution.py:23
  129.0 0.9 fusion.57
  129.9 0.1 slice_bitcast_fusion.32
  130.0 0.1 pad_slice_fusion
  130.1 0.1 slice.338
  130.2 0.1 slice.344
  130.4 0.1 fusion.56
  130.5 0.1 fusion.8
  130.6 0.1 maximum_bitcast_fusion
  130.7 1.2 copy.161
  131.9 1.4 %copy.162 = bf16[2,64,12,256]{3,1,2,0:T(8,128)(2,1)} copy(bf16[2,64,12,256]{1,3,2,0:T(8,128)(2,1)S(1)} %bitcast.295) | data formatting | bytes 1572864 | tf_op jit(solution)/shard_map/convert_element_type | solution.py:104
  (26 shorter events, 0.5 us)
Async XLA Ops:
  6.5 112.8 %copy-start = (bf16[27,64,128]{2,1,0:T(8,128)(2,1)S(1)}, bf16[27,64,128]{2,1,0:T(8,128)(2,1)}, u32[]{:S(2)}) copy-start(bf16[27,64,128]{2,1,0:T(8,128)(2,1)} %param.7) | copy-start | bytes 1327108
  6.5 101.1 %all-gather.2.cloned.1.call-start = ((), (), s32[]{:S(2)}) async-start(), calls=%async_computation.1 | async-start | bytes 1880064 | tf_op jit(solution)/shard_map/all_gather | solution.py:92
  24.4 8.0 %collective-permute-start = (bf16[1,256,6,128]{3,1,2,0:T(8,128)(2,1)S(1)}, bf16[1,256,6,128]{3,1,2,0:T(8,128)(2,1)S(1)}, u32[]{:S(2)}, u32[]{:S(2)}) collective-permute-start(bf16[1,256,6,128]{3,1,2,0:T(8,128)(2,1)S(1)} %bitcast.296), channel_id=1, source_target_pairs={{0,1},{1,2},{2,3},{3,4},{4,5},{5,6},{6,7},{7,8},{8,9},{9,10},{10,1... | collective-permute-start | bytes 1179656 | tf_op jit(solution)/shard_map/ppermute | solution.py:12
  27.7 10.0 %collective-permute-start.1 = (bf16[1,256,6,128]{3,1,2,0:T(8,128)(2,1)S(1)}, bf16[1,256,6,128]{3,1,2,0:T(8,128)(2,1)S(1)}, u32[]{:S(2)}, u32[]{:S(2)}) collective-permute-start(bf16[1,256,6,128]{3,1,2,0:T(8,128)(2,1)S(1)} %bitcast.297), channel_id=1, source_target_pairs={{1,0},{2,1},{3,2},{4,3},{5,4},{6,5},{7,6},{8,7},{9,8},{10,9},{11,1... | collective-permute-start | bytes 1179656 | tf_op jit(solution)/shard_map/ppermute | solution.py:15
  93.8 18.1 %copy-start.1 = (f32[128]{0:T(128)S(1)}, f32[128]{0:T(128)}, u32[]{:S(2)}) copy-start(f32[128]{0:T(128)} %param.6) | copy-start | bytes 1540
  121.2 7.9 %collective-permute-start.2 = (bf16[1,128,6,128]{1,3,2,0:T(8,128)(2,1)S(1)}, bf16[1,128,6,128]{1,3,2,0:T(8,128)(2,1)S(1)}, u32[]{:S(2)}, u32[]{:S(2)}) collective-permute-start(bf16[1,128,6,128]{1,3,2,0:T(8,128)(2,1)S(1)} %bitcast.303), channel_id=1, source_target_pairs={{1,0},{2,1},{3,2},{4,3},{5,4},{6,5},{7,6},{8,7},{9,8},{10,9},{11,1... | collective-permute-start | bytes 589832 | tf_op jit(solution)/shard_map/ppermute | solution.py:23
Sparse Core Ops, SparseCore 0:
  29.8 39.9 all-gather.1
where the time goes:
time: 141 us; the launch traced here: 140 us
  local copies, waits for them, and re-layouts  76.6 us (54%)
  blocking collectives  17.9 us (13%)
  between operations  13.9 us (10%)
  waiting for transfers between devices  13.2 us (9%)
  matrix products  9.13 us (6%)
  starting transfers between devices  7.09 us (5%)
  other arithmetic  2.26 us (2%)
    another operation x2, local copies, waits for them, and re-layouts, conv_rows(): jnp.stack(taps, axis=2).reshape(count, chans * 27, wide_y * wide_z)  43.4 us
    all_to_all x1, blocking collectives, per_device(): lax.all_to_all(volume, 'gx', split_axis=0, concat_axis=1, tiled=True)  17.9 us
    dot_general x1, local copies, waits for them, and re-layouts, conv_rows(): jnp.einsum('fwh,wb->fbh', patch_columns, flattened_patches, preferred_ele...  13.9 us
    unnamed x32, local copies, waits for them, and re-layouts  10.8 us
    dot_general x1, matrix products, conv_rows(): jnp.einsum('fwh,wb->fbh', patch_columns, flattened_patches, preferred_ele...  7.43 us
    ppermute x1, waiting for transfers between devices, extended(): lax.ppermute(lax.slice_in_dim(block, 0, width, axis=dim), axis, backward)  5.28 us
    ppermute x1, waiting for transfers between devices, from_behind(): return lax.ppermute(block, axis, route)  5.16 us
    ppermute x1, starting transfers between devices, extended(): lax.ppermute(lax.slice_in_dim(block, block.shape[dim] - width, None, axis...  3.24 us
  transfers between devices with their start and end apart: 4, of which 3 were waited for; matrix products, arithmetic and copies ran while one was open for 50% of the time, Pallas kernels for 0%

commit v1 on v0

--- a/solution.py
+++ b/solution.py
@@ -83,10 +83,18 @@
 
 
 def per_device(volume, conv_weight, conv_bias, tconv_weight):
+
+    def unite_tasks_up(view):
+        val = jax.lax.psum(1, "gx")
+        b_now = jnp.split(view, val, axis=0)
+        v_now = jnp.stack(b_now, axis=0)
+        found_now = jax.lax.all_to_all(v_now, "gx", 0, 0)
+        return jnp.concatenate(found_now, axis=1)
+
     wide_x, wide_y, wide_z = (volume.shape[0], volume.shape[2], volume.shape[3])
     rows = wide_x // lax.axis_size("gx")
     cout = conv_weight.shape[2]
-    local = lax.all_to_all(volume, "gx", split_axis=0, concat_axis=1, tiled=True)
+    local = unite_tasks_up(volume)
     widened_volume = extended(local, (("gx", 0),), 1)
     padded_volume = jnp.pad(widened_volume, ((0, 0), (0, 0), (1, 1), (1, 1)))
     summed = conv_rows(padded_volume, lax.all_gather(conv_weight, "gx", axis=0, tiled=True), rows)

time: 141 us -> 153 us (1.085)
  local copies, waits for them, and re-layouts: 76.6 us -> 88.6 us
    unnamed x32 -> x47, local copies, waits for them, and re-layouts: 10.8 us -> 22 us
  transfers between devices with their start and end apart: 4 -> 4, of which waited for: 3 -> 3; matrix products, arithmetic and copies ran while one was open for 50% -> 46% of each run, Pallas kernels for 0% -> 0%
where the time goes in v1:
time: 153 us; the launch traced here: 152 us
  local copies, waits for them, and re-layouts  88.6 us (58%)
  blocking collectives  17.5 us (11%)
  between operations  14 us (9%)
  waiting for transfers between devices  13.2 us (9%)
  matrix products  9.13 us (6%)
  starting transfers between devices  7.09 us (5%)
  other arithmetic  2.26 us (1%)
    another operation x2, local copies, waits for them, and re-layouts, conv_rows(): jnp.stack(taps, axis=2).reshape(count, chans * 27, wide_y * wide_z)  43.4 us
    unnamed x47, local copies, waits for them, and re-layouts  22 us
    all_to_all x1, blocking collectives, unite_tasks_up(): found_now = jax.lax.all_to_all(v_now, 'gx', 0, 0)  17.5 us
    dot_general x1, local copies, waits for them, and re-layouts, conv_rows(): jnp.einsum('fwh,wb->fbh', patch_columns, flattened_patches, preferred_ele...  13.9 us
    dot_general x1, matrix products, conv_rows(): jnp.einsum('fwh,wb->fbh', patch_columns, flattened_patches, preferred_ele...  7.43 us
    ppermute x1, waiting for transfers between devices, extended(): lax.ppermute(lax.slice_in_dim(block, 0, width, axis=dim), axis, backward)  5.28 us
    ppermute x1, waiting for transfers between devices, from_behind(): return lax.ppermute(block, axis, route)  5.16 us
    ppermute x1, starting transfers between devices, extended(): lax.ppermute(lax.slice_in_dim(block, block.shape[dim] - width, None, axis...  3.24 us
  transfers between devices with their start and end apart: 4, of which 3 were waited for; matrix products, arithmetic and copies ran while one was open for 46% of the time, Pallas kernels for 0%

profile of v1, /device:TPU:5, one launch (start us, length us, event | category | flops | bytes accessed | tf_op | source)
XLA Modules:
  0.0 151.8 jit_solution(498744873498025967)
XLA Ops:
  6.5 0.8 constant_dynamic-update-slice_fusion.15
  7.3 0.7 constant_dynamic-update-slice_fusion.14
  8.1 0.7 constant_dynamic-update-slice_fusion.13
  8.8 0.7 constant_dynamic-update-slice_fusion.12
  9.6 0.7 constant_dynamic-update-slice_fusion.11
  10.3 0.7 constant_dynamic-update-slice_fusion.10
  11.1 0.7 constant_dynamic-update-slice_fusion.9
  11.8 0.7 constant_dynamic-update-slice_fusion.8
  12.5 0.7 constant_dynamic-update-slice_fusion.7
  13.3 0.7 constant_dynamic-update-slice_fusion.6
  14.0 0.7 constant_dynamic-update-slice_fusion.5
  14.8 0.7 constant_dynamic-update-slice_fusion.4
  15.5 0.7 constant_dynamic-update-slice_fusion.3
  16.3 0.7 constant_dynamic-update-slice_fusion.2
  17.0 0.7 constant_dynamic-update-slice_fusion.1
  17.8 0.7 constant_dynamic-update-slice_fusion
  18.5 17.5 %all_to_all.5 = bf16[16,1,16,6,128]{4,2,3,1,0:T(8,128)(2,1)S(1)} all-to-all(bf16[16,1,16,6,128]{4,2,3,1,0:T(8,128)(2,1)S(1)} %constant_dynamic-update-slice_fusion), channel_id=1, replica_groups=mesh['groups'=2,'gx'=16] {'gx'}, dimensions={0} | all-to-all | bytes 786432 | tf_op jit(solution)/shard_map/all_to_all | solution.py:91
  36.1 3.2 %collective-permute-start = (bf16[1,256,6,128]{3,1,2,0:T(8,128)(2,1)S(1)}, bf16[1,256,6,128]{3,1,2,0:T(8,128)(2,1)S(1)}, u32[]{:S(2)}, u32[]{:S(2)}) collective-permute-start(bf16[1,256,6,128]{3,1,2,0:T(8,128)(2,1)S(1)} %bitcast.328), channel_id=1, source_target_pairs={{0,1},{1,2},{2,3},{3,4},{4,5},{5,6},{6,7},{7,8},{8,9},{9,10},{10,1... | collective-permute-start | bytes 1179656 | tf_op jit(solution)/shard_map/ppermute | solution.py:12
  39.3 1.9 %collective-permute-start.1 = (bf16[1,256,6,128]{3,1,2,0:T(8,128)(2,1)S(1)}, bf16[1,256,6,128]{3,1,2,0:T(8,128)(2,1)S(1)}, u32[]{:S(2)}, u32[]{:S(2)}) collective-permute-start(bf16[1,256,6,128]{3,1,2,0:T(8,128)(2,1)S(1)} %bitcast.329), channel_id=1, source_target_pairs={{1,0},{2,1},{3,2},{4,3},{5,4},{6,5},{7,6},{8,7},{9,8},{10,9},{11,1... | collective-permute-start | bytes 1179656 | tf_op jit(solution)/shard_map/ppermute | solution.py:15
  41.3 2.8 %collective-permute-done = bf16[1,256,6,128]{3,1,2,0:T(8,128)(2,1)S(1)} collective-permute-done((bf16[1,256,6,128]{3,1,2,0:T(8,128)(2,1)S(1)}, bf16[1,256,6,128]{3,1,2,0:T(8,128)(2,1)S(1)}, u32[]{:S(2)}, u32[]{:S(2)}) %collective-permute-start) | collective-permute-done | bytes 393248 | tf_op jit(solution)/shard_map/ppermute | solution.py:12
  44.0 5.3 %collective-permute-done.1 = bf16[1,256,6,128]{3,1,2,0:T(8,128)(2,1)S(1)} collective-permute-done((bf16[1,256,6,128]{3,1,2,0:T(8,128)(2,1)S(1)}, bf16[1,256,6,128]{3,1,2,0:T(8,128)(2,1)S(1)}, u32[]{:S(2)}, u32[]{:S(2)}) %collective-permute-start.1) | collective-permute-done | bytes 393248 | tf_op jit(solution)/shard_map/ppermute | solution.py:15
  49.3 1.7 %select_maximum_fusion = bf16[3,256,8,130]{3,1,2,0:T(8,128)(2,1)S(1)} fusion(bf16[1,256,6,128]{3,1,2,0:T(8,128)(2,1)S(1)} %collective-permute-done.1, bf16[1,256,6,128]{3,1,2,0:T(8,128)(2,1)S(1)} %bitcast.330, bf16[1,256,6,128]{3,1,2,0:T(8,128)(2,1)S(1)} %collective-permute-done), kind=kLoop, calls=%fused_computation.8 | loop fusion | flops 15175680 | bytes 2777088 | tf_op jit(solution)/shard_map/concatenate | solution.py:16
  51.1 0.2 fusion.31
  51.3 0.2 fusion.30
  51.6 0.1 fusion.29
  51.8 0.2 fusion.28
  52.0 0.1 fusion.27
  52.1 0.2 fusion.26
  52.3 0.2 fusion.25
  52.6 0.1 fusion.24
  52.7 0.2 fusion.23
  52.9 0.2 fusion.22
  53.4 0.2 fusion.20
  53.7 0.2 fusion.18
  53.9 0.2 fusion.17
  54.3 0.2 fusion.15
  54.5 0.2 fusion.14
  54.9 0.2 fusion.12
  55.3 0.2 fusion.10
  55.5 0.2 fusion.9
  55.8 43.2 %copy.127 = bf16[1,256,27,6,128]{4,3,2,1,0:T(8,128)(2,1)S(1)} copy(bf16[1,256,27,6,128]{4,1,3,2,0:T(8,128)(2,1)S(1)} %fusion.9) | data formatting | bytes 21233664 | tf_op jit(solution)/shard_map/stack | solution.py:69
  99.0 6.4 %copy.250 = bf16[864,8,6,128]{3,1,2,0:T(8,128)(2,1)} copy(bf16[864,8,6,128]{3,2,1,0:T(8,128)(2,1)S(1)} %bitcast.320) | data formatting | bytes 21233664
  105.4 13.9 %copy.128 = bf16[768,6912]{1,0:T(8,128)(2,1)} copy(bf16[768,6912]{0,1:T(8,128)(2,1)} %bitcast.321) | data formatting | bytes 21233664 | tf_op jit(solution)/shard_map/fwh,wb->fbh/dot_general | solution.py:71
  119.3 2.7 %copy.129 = bf16[256,27,128]{2,1,0:T(8,128)(2,1)S(1)} copy(bf16[256,27,128]{2,0,1:T(8,128)(2,1)} %all-gather.2.cloned.1.call-done) | data formatting | bytes 3538944 | tf_op jit(solution)/shard_map/all_gather | solution.py:100
  122.0 1.6 %reshape.120 = bf16[6912,128,1]{1,0,2:T(8,128)(2,1)} reshape(bf16[256,27,128]{2,1,0:T(8,128)(2,1)S(1)} %copy.129) | data formatting | bytes 3538944 | tf_op jit(solution)/shard_map/reshape | solution.py:70
  123.5 7.4 %fusion.7 = bf16[6,128,128]{2,1,0:T(8,128)(2,1)S(1)} fusion(bf16[6,128,6912]{2,1,0:T(8,128)(2,1)} %bitcast.324, bf16[6912,128,1]{1,0,2:T(8,128)(2,1)} %reshape.120, f32[128]{0:T(128)S(1)} %copy-done.1), kind=kOutput, calls=%fused_computation.15 | convolution fusion | flops 1359249408 | bytes 12583424 | tf_op jit(solution)/shard_map/fwh,wb->fbh/dot_general | solution.py:71
  130.9 0.9 fusion.59
  131.8 0.4 fusion.65
  132.3 0.1 slice.310
  132.5 0.1 slice.316
  132.7 0.1 pad_slice_fusion.2
  132.8 1.9 %collective-permute-start.2 = (bf16[1,128,6,128]{1,3,2,0:T(8,128)(2,1)S(1)}, bf16[1,128,6,128]{1,3,2,0:T(8,128)(2,1)S(1)}, u32[]{:S(2)}, u32[]{:S(2)}) collective-permute-start(bf16[1,128,6,128]{1,3,2,0:T(8,128)(2,1)S(1)} %bitcast.335), channel_id=1, source_target_pairs={{1,0},{2,1},{3,2},{4,3},{5,4},{6,5},{7,6},{8,7},{9,8},{10,9},{11,1... | collective-permute-start | bytes 589832 | tf_op jit(solution)/shard_map/ppermute | solution.py:23
  134.7 0.1 slice.324
  134.9 0.1 slice.330
  135.1 0.1 pad_slice_fusion.1
  135.5 5.2 %collective-permute-done.2 = bf16[1,128,6,128]{1,3,2,0:T(8,128)(2,1)S(1)} collective-permute-done((bf16[1,128,6,128]{1,3,2,0:T(8,128)(2,1)S(1)}, bf16[1,128,6,128]{1,3,2,0:T(8,128)(2,1)S(1)}, u32[]{:S(2)}, u32[]{:S(2)}) %collective-permute-start.2) | collective-permute-done | bytes 196640 | tf_op jit(solution)/shard_map/ppermute | solution.py:23
  140.7 0.9 fusion.57
  141.6 0.1 pad_slice_fusion
  141.8 0.1 slice.338
  141.9 0.1 slice.344
  142.0 0.1 fusion.56
  142.1 0.1 fusion.8
  142.4 1.2 copy.159
  143.5 1.4 copy.160
  (42 shorter events, 1.5 us)
Async XLA Ops:
  6.5 124.4 %copy-start = (bf16[27,64,128]{2,1,0:T(8,128)(2,1)S(1)}, bf16[27,64,128]{2,1,0:T(8,128)(2,1)}, u32[]{:S(2)}) copy-start(bf16[27,64,128]{2,1,0:T(8,128)(2,1)} %param.7) | copy-start | bytes 1327108
  6.5 112.8 %all-gather.2.cloned.1.call-start = ((), (), s32[]{:S(2)}) async-start(), calls=%async_computation.1 | async-start | bytes 1880064 | tf_op jit(solution)/shard_map/all_gather | solution.py:100
  36.1 8.0 %collective-permute-start = (bf16[1,256,6,128]{3,1,2,0:T(8,128)(2,1)S(1)}, bf16[1,256,6,128]{3,1,2,0:T(8,128)(2,1)S(1)}, u32[]{:S(2)}, u32[]{:S(2)}) collective-permute-start(bf16[1,256,6,128]{3,1,2,0:T(8,128)(2,1)S(1)} %bitcast.328), channel_id=1, source_target_pairs={{0,1},{1,2},{2,3},{3,4},{4,5},{5,6},{6,7},{7,8},{8,9},{9,10},{10,1... | collective-permute-start | bytes 1179656 | tf_op jit(solution)/shard_map/ppermute | solution.py:12
  39.3 10.0 %collective-permute-start.1 = (bf16[1,256,6,128]{3,1,2,0:T(8,128)(2,1)S(1)}, bf16[1,256,6,128]{3,1,2,0:T(8,128)(2,1)S(1)}, u32[]{:S(2)}, u32[]{:S(2)}) collective-permute-start(bf16[1,256,6,128]{3,1,2,0:T(8,128)(2,1)S(1)} %bitcast.329), channel_id=1, source_target_pairs={{1,0},{2,1},{3,2},{4,3},{5,4},{6,5},{7,6},{8,7},{9,8},{10,9},{11,1... | collective-permute-start | bytes 1179656 | tf_op jit(solution)/shard_map/ppermute | solution.py:15
  105.4 18.1 %copy-start.1 = (f32[128]{0:T(128)S(1)}, f32[128]{0:T(128)}, u32[]{:S(2)}) copy-start(f32[128]{0:T(128)} %param.6) | copy-start | bytes 1540
  132.8 7.9 %collective-permute-start.2 = (bf16[1,128,6,128]{1,3,2,0:T(8,128)(2,1)S(1)}, bf16[1,128,6,128]{1,3,2,0:T(8,128)(2,1)S(1)}, u32[]{:S(2)}, u32[]{:S(2)}) collective-permute-start(bf16[1,128,6,128]{1,3,2,0:T(8,128)(2,1)S(1)} %bitcast.335), channel_id=1, source_target_pairs={{1,0},{2,1},{3,2},{4,3},{5,4},{6,5},{7,6},{8,7},{9,8},{10,9},{11,1... | collective-permute-start | bytes 589832 | tf_op jit(solution)/shard_map/ppermute | solution.py:23
Sparse Core Ops, SparseCore 0:
  41.4 39.9 all-gather.1
